TPU v7x, 256 devices: a whole 4x4x8 slice. The times are simulated.
256 devices in a mesh: dp: 4 (over x), depth: 2 (over y_hi), tensor: 32 (over y_lo, z, core).
Axes of the slice: x: 4, y: 4 (y_hi: 2, y_lo: 2; y = y_hi * 2 + y_lo), z: 8, core: 2. Of those that a mesh axis runs over, the one named last changes fastest.
Arguments:
- text: bfloat16 [512, 8192], P(('dp', 'tensor')), may hold values from -6 to 6
- vision: bfloat16 [1024, 8192], P(('dp', 'depth'), 'tensor'), may hold values from -6 to 6
- query_weight: bfloat16 [2, 8192, 8192], P('depth', None, 'tensor'), may hold values from -0.0625 to 0.0625
- key_weight: bfloat16 [2, 8192, 1024], P('depth', 'tensor'), may hold values from -0.0625 to 0.0625
- value_weight: bfloat16 [2, 8192, 1024], P('depth', 'tensor'), may hold values from -0.0625 to 0.0625
- out_weight: bfloat16 [2, 8192, 8192], P('depth', 'tensor'), may hold values from -0.25 to 0.25
- gate: float32 [2], P('depth'), may hold values from 0.5 to 1.5
- cotangent: bfloat16 [512, 8192], P(('dp', 'tensor')), may hold values from -0.75 to 0.75
- tile_table: int32 [4, 8, 4], P('dp'), may hold values 0 or 1
- vision_tiles: int32 [4], P('dp'), may hold values from 1 to 4
- text_lengths: int32 [4], P('dp'), may hold values from 64 to 128
Outputs:
- hidden_states: bfloat16 [2, 512, 8192], P('depth', ('dp', 'tensor'))
- text_grads: bfloat16 [2, 512, 8192], P('depth', ('dp', 'tensor'))
- vision_grad: float32 [1024, 8192], P(('dp', 'depth'), 'tensor')
- key_weight_grad: float32 [2, 8192, 1024], P('depth', 'tensor', 'dp')
- value_weight_grad: float32 [2, 8192, 1024], P('depth', 'tensor', 'dp')
All inputs are finite; a program needn't handle non-finite values. No bound on the sum of `tile_table` on one device may be relied on, other than what follows from the above.
Results may differ from a plain program's by a relative error of at most 0.034.
Values may be sent and summed in bfloat16 or wider, within the bound.
No kernel may reach another device: no remote copies, remote signals or barrier semaphores. Data moves between devices by JAX's collectives and lax.ppermute only.
A program may use at most 128 MiB of HBM per device.

v0:
```python
import math
import jax
import jax.numpy as jnp
from jax import lax
from jax.sharding import PartitionSpec as P

HD = 128
QGROUP = 8
SEQ = 128
TBLK = 16
TILES = 4
TILE_ROWS = 64
VIS = 256


def shifted(value, axis, steps):
    count = lax.axis_size(axis)
    first, last = (max(0, -steps), min(count, count - steps))
    return lax.ppermute(value, axis, [(source, source + steps) for source in range(first, last)])


def normalize(values, epsilon):
    return values * lax.rsqrt(jnp.mean(values * values, axis=-1, keepdims=True) + epsilon)


def norm_back(values, upstream, epsilon):
    inv_rms = lax.rsqrt(jnp.mean(values * values, axis=-1, keepdims=True) + epsilon)
    normed = values * inv_rms
    return inv_rms * (upstream - normed * jnp.mean(upstream * normed, axis=-1, keepdims=True))


def allowed_mask(table, tile_count, text_count):
    tile_ok = jnp.arange(TILES, dtype=jnp.int32) < tile_count
    block_ok = (table > 0) & tile_ok[None, :]
    full_mask = jnp.broadcast_to(
        block_ok[:, None, :, None], (SEQ // TBLK, TBLK, TILES, TILE_ROWS)
    ).reshape(SEQ, VIS)
    row_ok = jnp.arange(SEQ, dtype=jnp.int32) < text_count
    return full_mask & row_ok[:, None]


def token_rows(shard, transform):
    return transform(lax.all_gather(shard, "tensor", axis=0, tiled=True), jnp.int32(0))


def token_sums(term, shard_rows):
    return lax.psum_scatter(
        term(jnp.int32(0), shard_rows * lax.axis_size("tensor")).astype(jnp.bfloat16),
        "tensor",
        scatter_dimension=0,
        tiled=True,
    ).astype(jnp.float32)


def kv_totals(keys_part, values_part):
    return lax.psum((keys_part, values_part), "tensor")


def per_device(
    text,
    vision,
    query_weight,
    key_weight,
    value_weight,
    out_weight,
    gate,
    cotangent,
    tile_table,
    vision_tiles,
    text_lengths,
):
    layers = lax.axis_size("depth")
    section_index = lax.axis_index("depth")
    tensor_index = lax.axis_index("tensor")
    w_query = query_weight[0]
    w_key = key_weight[0]
    w_value = value_weight[0]
    w_out = out_weight[0]
    gate_value = jnp.tanh(gate[0])
    local_width = w_query.shape[1]
    local_heads = local_width // HD
    kv_width = w_key.shape[1]
    kv_heads = kv_width // HD
    shard_rows = text.shape[0]
    inv_sqrt = 1.0 / math.sqrt(HD)
    kv_group = tensor_index * local_heads // QGROUP
    allowed = allowed_mask(tile_table[0], vision_tiles[0], text_lengths[0])
    row_live = jnp.any(allowed, axis=-1).astype(jnp.float32)
    vis_full = lax.all_gather(vision, "depth", axis=0, tiled=True)
    keys_part = jnp.dot(vis_full, w_key, preferred_element_type=jnp.float32)
    values_part = jnp.dot(vis_full, w_value, preferred_element_type=jnp.float32)
    keys_pre, values_pre = kv_totals(keys_part, values_part)
    keys_cast = (
        normalize(keys_pre.reshape(VIS, kv_heads, HD), 1e-06)
        .astype(jnp.bfloat16)
        .reshape(VIS, kv_width)
    )
    values_cast = values_pre.astype(jnp.bfloat16)
    key_group = lax.dynamic_slice_in_dim(keys_cast, kv_group * HD, HD, 1)
    value_group = lax.dynamic_slice_in_dim(values_cast, kv_group * HD, HD, 1)
    current = text
    for layer_at in range(layers):

        def project(rows_in, offset):
            normed = normalize(rows_in.astype(jnp.float32), 1e-05).astype(jnp.bfloat16)
            return jnp.dot(normed, w_query, preferred_element_type=jnp.float32)

        layer_queries = token_rows(current, project).reshape(SEQ, local_heads, HD)
        layer_query_cast = normalize(layer_queries, 1e-06).astype(jnp.bfloat16)
        scores = (
            jnp.einsum(
                "shd,vd->hsv", layer_query_cast, key_group, preferred_element_type=jnp.float32
            )
            * inv_sqrt
        )
        expd = jnp.where(allowed[None], jnp.exp(scores), 0.0)
        layer_probs = expd / (
            jnp.sum(expd, axis=-1, keepdims=True) + (1.0 - row_live)[None, :, None]
        )
        layer_probs_cast = layer_probs.astype(jnp.bfloat16)
        mixed = jnp.einsum(
            "hsv,vd->shd", layer_probs_cast, value_group, preferred_element_type=jnp.float32
        )
        mixed_cast = mixed.astype(jnp.bfloat16).reshape(SEQ, local_width)

        def out_term(offset, number):
            return jnp.dot(mixed_cast, w_out, preferred_element_type=jnp.float32)

        attended = token_sums(out_term, shard_rows)
        outputs = (current.astype(jnp.float32) + gate_value * attended).astype(jnp.bfloat16)
        outputs, kept = (outputs, (layer_queries, layer_query_cast, layer_probs, layer_probs_cast))
        chosen = section_index == layer_at
        if layer_at == 0:
            saved_in, saved_out, saved_kept = (current, outputs, kept)
        else:
            saved_in = jnp.where(chosen, current, saved_in)
            saved_out = jnp.where(chosen, outputs, saved_out)
            saved_kept = jax.tree.map(
                lambda fresh, older: jnp.where(chosen, fresh, older), kept, saved_kept
            )
        if layer_at + 1 < layers:
            current = shifted(outputs, "depth", 1)
    upstream = cotangent
    for layer_at in reversed(range(layers)):
        queries, query_cast, probs, probs_cast = saved_kept
        scaled = (gate_value * upstream.astype(jnp.float32)).astype(jnp.bfloat16)

        def back_project(rows_in, offset):
            return jnp.einsum("sd,kd->sk", rows_in, w_out, preferred_element_type=jnp.float32)

        dmixed = token_rows(scaled, back_project).astype(jnp.bfloat16).reshape(SEQ, local_heads, HD)
        dprobs = jnp.einsum("shd,vd->hsv", dmixed, value_group, preferred_element_type=jnp.float32)
        layer_dvalues = jnp.einsum(
            "hsv,shd->vd", probs_cast, dmixed, preferred_element_type=jnp.float32
        )
        dscores = (
            probs * (dprobs - jnp.sum(probs * dprobs, axis=-1, keepdims=True)) * inv_sqrt
        ).astype(jnp.bfloat16)
        dquery_hat = jnp.einsum(
            "hsv,vd->shd", dscores, key_group, preferred_element_type=jnp.float32
        )
        layer_dkeys_hat = jnp.einsum(
            "hsv,shd->vd", dscores, query_cast, preferred_element_type=jnp.float32
        )
        dquery = (
            norm_back(queries, dquery_hat, 1e-06).astype(jnp.bfloat16).reshape(SEQ, local_width)
        )

        def in_term(offset, number):
            return jnp.einsum("sk,dk->sd", dquery, w_query, preferred_element_type=jnp.float32)

        dnormed = token_sums(in_term, shard_rows)
        dinputs = (
            upstream.astype(jnp.float32) + norm_back(saved_in.astype(jnp.float32), dnormed, 1e-05)
        ).astype(jnp.bfloat16)
        dinputs, kv_grads = (dinputs, (layer_dkeys_hat, layer_dvalues))
        chosen = section_index == layer_at
        if layer_at == layers - 1:
            saved_grad, saved_kv = (dinputs, kv_grads)
        else:
            saved_grad = jnp.where(chosen, dinputs, saved_grad)
            saved_kv = jax.tree.map(
                lambda fresh, older: jnp.where(chosen, fresh, older), kv_grads, saved_kv
            )
        if layer_at > 0:
            upstream = shifted(dinputs, "depth", -1)
    dkeys_hat, dvalues = saved_kv
    one_hot = (jnp.arange(kv_heads, dtype=jnp.int32) == kv_group).astype(jnp.float32)
    dkeys_full = (dkeys_hat[:, None, :] * one_hot[None, :, None]).reshape(VIS, kv_width)
    dvalues_full = (dvalues[:, None, :] * one_hot[None, :, None]).reshape(VIS, kv_width)
    dkeys_total, dvalues_total = kv_totals(dkeys_full, dvalues_full)
    dkeys_cast = (
        norm_back(
            keys_pre.reshape(VIS, kv_heads, HD), dkeys_total.reshape(VIS, kv_heads, HD), 1e-06
        )
        .astype(jnp.bfloat16)
        .reshape(VIS, kv_width)
    )
    dvalues_cast = dvalues_total.astype(jnp.bfloat16)
    dvision_part = jnp.einsum(
        "vc,dc->vd", dkeys_cast, w_key, preferred_element_type=jnp.float32
    ) + jnp.einsum("vc,dc->vd", dvalues_cast, w_value, preferred_element_type=jnp.float32)
    dvision = lax.psum_scatter(dvision_part, "depth", scatter_dimension=0, tiled=True)
    dkey_part = jnp.einsum("vd,vc->dc", vis_full, dkeys_cast, preferred_element_type=jnp.float32)
    dvalue_part = jnp.einsum(
        "vd,vc->dc", vis_full, dvalues_cast, preferred_element_type=jnp.float32
    )
    dkey_grad, dvalue_grad = (
        lax.psum_scatter(dkey_part, "dp", scatter_dimension=1, tiled=True),
        lax.psum_scatter(dvalue_part, "dp", scatter_dimension=1, tiled=True),
    )
    return (saved_out[None], saved_grad[None], dvision, dkey_grad[None], dvalue_grad[None])


def solution(mesh):
    in_specs = (
        P(("dp", "tensor"), None),
        P(("dp", "depth"), "tensor"),
        P("depth", None, "tensor"),
        P("depth", "tensor", None),
        P("depth", "tensor", None),
        P("depth", "tensor", None),
        P("depth"),
        P(("dp", "tensor"), None),
        P("dp", None, None),
        P("dp"),
        P("dp"),
    )
    out_specs = (
        P("depth", ("dp", "tensor"), None),
        P("depth", ("dp", "tensor"), None),
        P(("dp", "depth"), "tensor"),
        P("depth", "tensor", "dp"),
        P("depth", "tensor", "dp"),
    )
    return jax.shard_map(
        per_device, mesh=mesh, in_specs=in_specs, out_specs=out_specs, check_vma=False
    )
```

profile of v0, /device:TPU:1, one launch (start us, length us, event | category | flops | bytes accessed | tf_op | source)
XLA Modules:
  0.0 1562.4 jit_solution(4551209075161023634)
XLA Ops:
  7.2 6.5 all_gather.15
  15.8 6.5 copy.96
  27.3 118.3 %all-reduce.22 = bf16[256,1024]{1,0:T(8,128)(2,1)} all-reduce(f32[256,1024]{1,0:T(8,128)S(1)} %fusion.54), channel_id=1, replica_groups=mesh['dp'=4,'depth'=2,'tensor'=32] {'tensor'}, use_global_device_ids=true, to_apply=%region_0.1 | all-reduce | flops 262144 | bytes 1572864 | tf_op jit(solution)/shard_map/psum | solution.py:56
  145.6 98.3 %all-reduce.13.cloned.1.call-done = f32[256,1024]{1,0:T(8,128)} async-done(((f32[256,1024]{1,0:T(8,128)}), f32[256,1024]{1,0:T(8,128)}) %all-reduce.13.cloned.1.call-update) | async-done | bytes 1048592 | tf_op jit(solution)/shard_map/psum | solution.py:56
  248.2 61.3 %all-gather.9.cloned.1.call-done = bf16[32,4,8192]{2,1,0:T(4,128)(2,1)} async-done(((bf16[1,4,8192]{2,1,0:T(4,128)(2,1)}), bf16[32,4,8192]{2,1,0:T(4,128)(2,1)}) %all-gather.9.cloned.1.call-update) | async-done | bytes 2097168 | tf_op jit(solution)/shard_map/all_gather | solution.py:43
  309.5 4.3 reshape.252
  328.2 224.7 %all-reduce.17.cloned.1.call-done = bf16[128,8192]{1,0:T(8,128)(2,1)} async-done(((bf16[128,8192]{1,0:T(8,128)(2,1)}), bf16[128,8192]{1,0:T(8,128)(2,1)}) %all-reduce.17.cloned.1.call-update) | async-done | bytes 2097168
  553.9 4.3 collective-permute-start
  560.5 58.4 %all-gather.13.cloned.1.call-done = bf16[32,4,8192]{2,1,0:T(4,128)(2,1)} async-done(((bf16[1,4,8192]{2,1,0:T(4,128)(2,1)}), bf16[32,4,8192]{2,1,0:T(4,128)(2,1)}) %all-gather.13.cloned.1.call-update) | async-done | bytes 2097168 | tf_op jit(solution)/shard_map/all_gather | solution.py:43
  622.8 4.4 fusion.43
  628.9 56.7 %all-gather.11.cloned.1.call-done = bf16[32,4,8192]{2,1,0:T(4,128)(2,1)} async-done(((bf16[1,4,8192]{2,1,0:T(4,128)(2,1)}), bf16[32,4,8192]{2,1,0:T(4,128)(2,1)}) %all-gather.11.cloned.1.call-update) | async-done | bytes 2097168 | tf_op jit(solution)/shard_map/all_gather | solution.py:43
  685.5 4.3 reshape.253
  700.5 5.1 convolution_convert_fusion.1
  705.9 226.9 %all-reduce.19.cloned.1.call-done = bf16[128,8192]{1,0:T(8,128)(2,1)} async-done(((bf16[128,8192]{1,0:T(8,128)(2,1)}), bf16[128,8192]{1,0:T(8,128)(2,1)}) %all-reduce.19.cloned.1.call-update) | async-done | bytes 2097168
  936.3 5.2 collective-permute-done.1
  945.3 59.2 %all-gather.15.cloned.1.call-done = bf16[32,4,8192]{2,1,0:T(4,128)(2,1)} async-done(((bf16[1,4,8192]{2,1,0:T(4,128)(2,1)}), bf16[32,4,8192]{2,1,0:T(4,128)(2,1)}) %all-gather.15.cloned.1.call-update) | async-done | bytes 2097168 | tf_op jit(solution)/shard_map/all_gather | solution.py:43
  1008.5 4.4 fusion.40
  1018.3 113.1 %all-reduce.23 = bf16[256,1024]{1,0:T(8,128)(2,1)S(1)} all-reduce(f32[256,1024]{1,0:T(8,128)} %get-tuple-element.29), channel_id=1, replica_groups=mesh['dp'=4,'depth'=2,'tensor'=32] {'tensor'}, use_global_device_ids=true, to_apply=%region_24.25 | all-reduce | flops 262144 | bytes 1572864 | tf_op jit(solution)/shard_map/psum | solution.py:56
  1132.8 109.7 %all-reduce.15.cloned.1.call-done = f32[256,1024]{1,0:T(8,128)} async-done(((f32[256,1024]{1,0:T(8,128)}), f32[256,1024]{1,0:T(8,128)}) %all-reduce.15.cloned.1.call-update) | async-done | bytes 1048592 | tf_op jit(solution)/shard_map/psum | solution.py:56
  1255.3 5.0 convolution_convert_fusion
  1262.4 5.8 reduce-scatter.8.cloned.1.call-done
  1270.0 26.7 %reduce-scatter.6.cloned.1.call-done = f32[256,256]{0,1:T(8,128)} async-done(((f32[256,1024]{0,1:T(8,128)}), f32[256,256]{0,1:T(8,128)}) %reduce-scatter.6.cloned.1.call-update) | async-done | bytes 262160 | tf_op jit(solution)/shard_map/reduce_scatter | solution.py:209
  1298.5 237.2 %all-reduce.21.cloned.1.call-done = (bf16[128,8192]{1,0:T(8,128)(2,1)}, bf16[128,8192]{1,0:T(8,128)(2,1)}) async-done(((bf16[128,8192]{1,0:T(8,128)(2,1)}, bf16[128,8192]{1,0:T(8,128)(2,1)}), (bf16[128,8192]{1,0:T(8,128)(2,1)}, bf16[128,8192]{1,0:T(8,128)(2,1)})) %all-reduce.21.cloned.1.call-update) | async-done | bytes 4194320
  1538.8 16.8 %reduce-scatter.4.cloned.1.call-done = f32[128,256]{1,0:T(8,128)} async-done(((f32[256,256]{1,0:T(8,128)}), f32[128,256]{1,0:T(8,128)}) %reduce-scatter.4.cloned.1.call-update) | async-done | bytes 131088 | tf_op jit(solution)/shard_map/reduce_scatter | solution.py:203
  (170 shorter events, 81.9 us)
Async XLA Ops:
  7.2 236.7 %all-reduce.13.cloned.1.call-start = ((), (), s32[]{:S(2)}) async-start(), calls=%async_computation.3 | async-start | bytes 2097152 | tf_op jit(solution)/shard_map/psum | solution.py:56
  15.0 294.5 %all-gather.9.cloned.1.call-start = ((), (), s32[]{:S(2)}) async-start(), calls=%async_computation.8 | async-start | bytes 2162688 | tf_op jit(solution)/shard_map/all_gather | solution.py:43
  15.8 537.2 %all-reduce.17.cloned.1.call-start = ((), (), s32[]{:S(2)}) async-start(), calls=%async_computation.12 | async-start | bytes 4194304
  15.8 11.1 copy-start.8
  245.8 68.0 %copy-start.10 = (f32[256,8]{1,0:T(8,128)}, f32[256,8]{1,0:T(8,128)S(1)}, u32[]{:S(2)}) copy-start(f32[256,8]{1,0:T(8,128)S(1)} %add_rsqrt_fusion) | copy-start | bytes 24580
  323.3 229.6 %copy-start.15 = (bf16[4,8192]{1,0:T(4,128)(2,1)S(1)}, bf16[4,8192]{1,0:T(4,128)(2,1)}, u32[]{:S(2)}) copy-start(bf16[4,8192]{1,0:T(4,128)(2,1)} %param.11) | copy-start | bytes 196612
  325.5 293.4 %all-gather.13.cloned.1.call-start = ((), (), s32[]{:S(2)}) async-start(), calls=%async_computation.10 | async-start | bytes 2162688 | tf_op jit(solution)/shard_map/all_gather | solution.py:43
  326.9 358.6 %all-gather.11.cloned.1.call-start = ((), (), s32[]{:S(2)}) async-start(), calls=%async_computation.9 | async-start | bytes 2162688 | tf_op jit(solution)/shard_map/all_gather | solution.py:43
  553.9 143.1 %copy-start.20 = (bf16[4,8192]{1,0:T(4,128)(2,1)}, bf16[4,8192]{1,0:T(4,128)(2,1)S(1)}, u32[]{:S(2)}) copy-start(bf16[4,8192]{1,0:T(4,128)(2,1)S(1)} %add_convert_fusion.1) | copy-start | bytes 196612
  553.9 5.7 collective-permute-start
  560.2 372.6 %all-reduce.19.cloned.1.call-start = ((), (), s32[]{:S(2)}) async-start(), calls=%async_computation.13 | async-start | bytes 4194304
  700.5 233.5 %copy-start.25 = (bf16[4,8192]{1,0:T(4,128)(2,1)S(1)}, bf16[4,8192]{1,0:T(4,128)(2,1)}, u32[]{:S(2)}) copy-start(bf16[4,8192]{1,0:T(4,128)(2,1)} %param.18) | copy-start | bytes 196612
  700.5 241.9 %copy-start.27 = (bf16[128,2,128]{0,2,1:T(8,128)(2,1)S(1)}, bf16[128,2,128]{0,2,1:T(8,128)(2,1)}, u32[]{:S(2)}) copy-start(bf16[128,2,128]{0,2,1:T(8,128)(2,1)} %copy-done.26) | copy-start | bytes 196612
  705.6 298.8 %all-gather.15.cloned.1.call-start = ((), (), s32[]{:S(2)}) async-start(), calls=%async_computation.11 | async-start | bytes 2162688 | tf_op jit(solution)/shard_map/all_gather | solution.py:43
  935.0 77.8 %copy-start.22 = (bf16[4,8192]{1,0:T(4,128)(2,1)}, bf16[4,8192]{1,0:T(4,128)(2,1)S(1)}, u32[]{:S(2)}) copy-start(bf16[4,8192]{1,0:T(4,128)(2,1)S(1)} %fusion.69) | copy-start | bytes 196612
  935.0 6.5 collective-permute-start.1
  942.2 300.3 %all-reduce.15.cloned.1.call-start = ((), (), s32[]{:S(2)}) async-start(), calls=%async_computation.4 | async-start | bytes 2097152 | tf_op jit(solution)/shard_map/psum | solution.py:56
  1018.3 250.0 %reduce-scatter.8.cloned.1.call-start = ((), (), s32[]{:S(2)}) async-start(), calls=%async_computation.7 | async-start | bytes 1310720 | tf_op jit(solution)/shard_map/reduce_scatter | solution.py:210
  1132.8 163.9 %reduce-scatter.6.cloned.1.call-start = ((), (), s32[]{:S(2)}) async-start(), calls=%async_computation.6 | async-start | bytes 1310720 | tf_op jit(solution)/shard_map/reduce_scatter | solution.py:209
  1248.1 287.6 %all-reduce.21.cloned.1.call-start = ((), (), s32[]{:S(2)}) async-start(), calls=%async_computation.14 | async-start | bytes 8388608
  1260.3 276.6 %copy-start.18 = (bf16[4,8192]{1,0:T(4,128)(2,1)S(1)}, bf16[4,8192]{1,0:T(4,128)(2,1)}, u32[]{:S(2)}) copy-start(bf16[4,8192]{1,0:T(4,128)(2,1)} %copy-done.16) | copy-start | bytes 196612
  1260.3 276.6 %copy-start.21 = (bf16[4,8192]{1,0:T(4,128)(2,1)S(1)}, bf16[4,8192]{1,0:T(4,128)(2,1)}, u32[]{:S(2)}) copy-start(bf16[4,8192]{1,0:T(4,128)(2,1)} %copy-done.20) | copy-start | bytes 196612
  1260.3 276.6 %copy-start.23 = (bf16[4,8192]{1,0:T(4,128)(2,1)S(1)}, bf16[4,8192]{1,0:T(4,128)(2,1)}, u32[]{:S(2)}) copy-start(bf16[4,8192]{1,0:T(4,128)(2,1)} %copy-done.22) | copy-start | bytes 196612
  1260.3 295.2 %reduce-scatter.4.cloned.1.call-start = ((), (), s32[]{:S(2)}) async-start(), calls=%async_computation.5 | async-start | bytes 393216 | tf_op jit(solution)/shard_map/reduce_scatter | solution.py:203
  (21 other events, 84.5 us)
Sparse Core Ops, SparseCore 0:
  15.1 228.7 all-reduce.12
  245.9 63.5 all-gather.8
  325.6 227.2 all-reduce.16
  555.2 63.5 all-gather.12
  621.1 64.3 all-gather.10
  705.8 226.9 all-reduce.18
  942.4 62.0 all-gather.14
  1018.4 224.0 all-reduce.14
  1245.1 23.1 reduce-scatter.7
  1270.8 25.8 reduce-scatter.5
  1299.4 236.2 all-reduce.20
  1538.6 16.8 reduce-scatter.3
where the time goes:
time: 1560 us
  waiting for transfers between devices  1190 us (76%)
  blocking collectives  238 us (15%)
  matrix products  53.6 us (3%)
  local copies, waits for them, and re-layouts  35.6 us (2%)
  other arithmetic  22.3 us (1%)
  between operations  17.5 us (1%)
    unnamed x15, waiting for transfers between devices  690 us
    all_gather x4, waiting for transfers between devices, token_rows(): lax.all_gather(shard, 'tensor', axis=0, tiled=True)  235 us
    psum x2, blocking collectives, kv_totals(): return lax.psum((keys_part, values_part), 'tensor')  231 us
    psum x2, waiting for transfers between devices, kv_totals(): return lax.psum((keys_part, values_part), 'tensor')  208 us
  transfers between devices with their start and end apart: 14, of which 14 were waited for; matrix products, arithmetic and copies ran while one was open for 4% of the time, Pallas kernels for 0%

commit v1 on v0

--- a/solution.py
+++ b/solution.py
@@ -40,7 +40,12 @@
 
 
 def token_rows(shard, transform):
-    return transform(lax.all_gather(shard, "tensor", axis=0, tiled=True), jnp.int32(0))
+    return transform(
+        jnp.concatenate(
+            lax.all_to_all(jnp.stack([shard] * lax.axis_size("tensor")), "tensor", 0, 0), axis=0
+        ),
+        jnp.int32(0),
+    )
 
 
 def token_sums(term, shard_rows):

time: 1560 us -> 1460 us (0.936)
  waiting for transfers between devices: 1190 us -> 1020 us
  starting transfers between devices: 6.54 us -> 35.3 us
  blocking collectives: 238 us -> 262 us
    all_gather x4 -> x0, waiting for transfers between devices: 235 us -> none  [token_rows(): lax.all_gather(shard, 'tensor', axis=0, tiled=True)]
    all_to_all x0 -> x4, waiting for transfers between devices: none -> 85.2 us  [token_rows(): lax.all_to_all(jnp.stack([shard] * lax.axis_size('tensor')), 'tensor', 0, 0)]
    all_to_all x0 -> x4, starting transfers between devices: none -> 29 us  [token_rows(): lax.all_to_all(jnp.stack([shard] * lax.axis_size('tensor')), 'tensor', 0, 0)]
    psum x2, waiting for transfers between devices: 208 us -> 182 us  [kv_totals(): return lax.psum((keys_part, values_part), 'tensor')]
    psum x2, blocking collectives: 231 us -> 255 us  [kv_totals(): return lax.psum((keys_part, values_part), 'tensor')]
    unnamed x15 -> x11, waiting for transfers between devices: 690 us -> 698 us
  transfers between devices with their start and end apart: 14 -> 14, of which waited for: 14 -> 12; matrix products, arithmetic and copies ran while one was open for 4% -> 5% of each run, Pallas kernels for 0% -> 0%
where the time goes in v1:
time: 1460 us; the launch traced here: 1450 us
  waiting for transfers between devices  1020 us (70%)
  blocking collectives  262 us (18%)
  matrix products  52.3 us (4%)
  local copies, waits for them, and re-layouts  43.2 us (3%)
  starting transfers between devices  35.3 us (2%)
  other arithmetic  20.9 us (1%)
  between operations  17.6 us (1%)
    unnamed x11, waiting for transfers between devices  698 us
    psum x2, blocking collectives, kv_totals(): return lax.psum((keys_part, values_part), 'tensor')  255 us
    psum x2, waiting for transfers between devices, kv_totals(): return lax.psum((keys_part, values_part), 'tensor')  182 us
    all_to_all x4, waiting for transfers between devices, token_rows(): lax.all_to_all(jnp.stack([shard] * lax.axis_size('tensor')), 'tensor', 0, 0)  85.2 us
  transfers between devices with their start and end apart: 14, of which 12 were waited for; matrix products, arithmetic and copies ran while one was open for 5% of the time, Pallas kernels for 0%

profile of v1, /device:TPU:1, one launch (start us, length us, event | category | flops | bytes accessed | tf_op | source)
XLA Modules:
  0.0 1453.2 jit_solution(9643870707142028241)
XLA Ops:
  7.2 6.5 all_gather.3
  17.3 11.6 all-to-all-start
  33.4 6.5 copy.96
  42.7 142.6 %all-reduce.22 = bf16[256,1024]{1,0:T(8,128)(2,1)} all-reduce(f32[256,1024]{1,0:T(8,128)} %fusion.50), channel_id=1, replica_groups=mesh['dp'=4,'depth'=2,'tensor'=32] {'tensor'}, use_global_device_ids=true, to_apply=%region_0.1 | all-reduce | flops 262144 | bytes 1572864 | tf_op jit(solution)/shard_map/psum | solution.py:61
  185.3 75.0 %all-reduce.13.cloned.1.call-done = f32[256,1024]{1,0:T(8,128)} async-done(((f32[256,1024]{1,0:T(8,128)}), f32[256,1024]{1,0:T(8,128)}) %all-reduce.13.cloned.1.call-update) | async-done | bytes 1048592 | tf_op jit(solution)/shard_map/psum | solution.py:61
  268.4 5.9 all-to-all-start.2
  291.2 234.1 %all-reduce.17.cloned.1.call-done = bf16[128,8192]{1,0:T(8,128)(2,1)} async-done(((bf16[128,8192]{1,0:T(8,128)(2,1)}), bf16[128,8192]{1,0:T(8,128)(2,1)}) %all-reduce.17.cloned.1.call-update) | async-done | bytes 2097168
  526.3 4.5 collective-permute-start
  534.2 5.3 all-to-all-start.1
  543.6 4.4 fusion.39
  550.3 38.7 %all-to-all-done.1 = bf16[32,4,8192]{2,1,0:T(4,128)(2,1)S(1)} async-done(((bf16[32,4,8192]{2,1,0:T(4,128)(2,1)}), bf16[32,4,8192]{2,1,0:T(4,128)(2,1)S(1)}, u32[]{:S(2)}, u32[]{:S(2)}) %all-to-all-start.1) | async-done | bytes 2097184 | tf_op jit(solution)/shard_map/all_to_all | solution.py:45
  601.4 5.0 convolution_convert_fusion.1
  607.5 226.9 %all-reduce.19.cloned.1.call-done = bf16[128,8192]{1,0:T(8,128)(2,1)} async-done(((bf16[128,8192]{1,0:T(8,128)(2,1)}), bf16[128,8192]{1,0:T(8,128)(2,1)}) %all-reduce.19.cloned.1.call-update) | async-done | bytes 2097168
  837.9 5.2 collective-permute-done.1
  846.0 6.1 all-to-all-start.3
  855.0 46.6 %all-to-all-done.3 = bf16[32,4,8192]{2,1,0:T(4,128)(2,1)} async-done(((bf16[32,4,8192]{2,1,0:T(4,128)(2,1)}), bf16[32,4,8192]{2,1,0:T(4,128)(2,1)}, u32[]{:S(2)}, u32[]{:S(2)}) %all-to-all-start.3) | async-done | bytes 2097184 | tf_op jit(solution)/shard_map/all_to_all | solution.py:45
  912.1 112.6 %all-reduce.23 = bf16[256,1024]{1,0:T(8,128)(2,1)S(1)} all-reduce(f32[256,1024]{1,0:T(8,128)S(1)} %get-tuple-element.29), channel_id=1, replica_groups=mesh['dp'=4,'depth'=2,'tensor'=32] {'tensor'}, use_global_device_ids=true, to_apply=%region_24.25 | all-reduce | flops 262144 | bytes 1572864 | tf_op jit(solution)/shard_map/psum | solution.py:61
  1026.4 106.9 %all-reduce.15.cloned.1.call-done = f32[256,1024]{1,0:T(8,128)} async-done(((f32[256,1024]{1,0:T(8,128)}), f32[256,1024]{1,0:T(8,128)}) %all-reduce.15.cloned.1.call-update) | async-done | bytes 1048592 | tf_op jit(solution)/shard_map/psum | solution.py:61
  1139.8 4.3 convolution_convert_fusion.2
  1145.5 5.1 convolution_convert_fusion
  1152.1 6.9 reduce-scatter.8.cloned.1.call-done
  1160.7 26.7 %reduce-scatter.6.cloned.1.call-done = f32[256,256]{0,1:T(8,128)} async-done(((f32[256,1024]{0,1:T(8,128)}), f32[256,256]{0,1:T(8,128)}) %reduce-scatter.6.cloned.1.call-update) | async-done | bytes 262160 | tf_op jit(solution)/shard_map/reduce_scatter | solution.py:214
  1189.2 237.3 %all-reduce.21.cloned.1.call-done = (bf16[128,8192]{1,0:T(8,128)(2,1)}, bf16[128,8192]{1,0:T(8,128)(2,1)}) async-done(((bf16[128,8192]{1,0:T(8,128)(2,1)}, bf16[128,8192]{1,0:T(8,128)(2,1)}), (bf16[128,8192]{1,0:T(8,128)(2,1)}, bf16[128,8192]{1,0:T(8,128)(2,1)})) %all-reduce.21.cloned.1.call-update) | async-done | bytes 4194320
  1429.5 16.9 %reduce-scatter.4.cloned.1.call-done = f32[128,256]{1,0:T(8,128)} async-done(((f32[256,256]{1,0:T(8,128)}), f32[128,256]{1,0:T(8,128)}) %reduce-scatter.4.cloned.1.call-update) | async-done | bytes 131088 | tf_op jit(solution)/shard_map/reduce_scatter | solution.py:208
  (196 shorter events, 94.3 us)
Async XLA Ops:
  7.2 253.1 %all-reduce.13.cloned.1.call-start = ((), (), s32[]{:S(2)}) async-start(), calls=%async_computation.7 | async-start | bytes 2097152 | tf_op jit(solution)/shard_map/psum | solution.py:61
  17.3 248.8 %all-to-all-start = ((bf16[32,4,8192]{2,1,0:T(4,128)(2,1)}), bf16[32,4,8192]{2,1,0:T(4,128)(2,1)S(1)}, u32[]{:S(2)}, u32[]{:S(2)}) async-start(bf16[32,4,8192]{2,1,0:T(4,128)(2,1)} %stack.8), calls=%async_computation | async-start | bytes 4194304 | tf_op jit(solution)/shard_map/all_to_all | solution.py:45
  268.4 262.4 %all-to-all-start.2 = ((bf16[32,4,8192]{2,1,0:T(4,128)(2,1)}), bf16[32,4,8192]{2,1,0:T(4,128)(2,1)}, u32[]{:S(2)}, u32[]{:S(2)}) async-start(bf16[32,4,8192]{2,1,0:T(4,128)(2,1)} %stack.10), calls=%async_computation.2 | async-start | bytes 4194304 | tf_op jit(solution)/shard_map/all_to_all | solution.py:45
  274.4 250.9 %all-reduce.17.cloned.1.call-start = ((), (), s32[]{:S(2)}) async-start(), calls=%async_computation.12 | async-start | bytes 4194304
  289.3 236.0 %copy-start.21 = (bf16[4,8192]{1,0:T(4,128)(2,1)S(1)}, bf16[4,8192]{1,0:T(4,128)(2,1)}, u32[]{:S(2)}) copy-start(bf16[4,8192]{1,0:T(4,128)(2,1)} %param.11) | copy-start | bytes 196612
  526.3 5.7 collective-permute-start
  534.2 54.7 %all-to-all-start.1 = ((bf16[32,4,8192]{2,1,0:T(4,128)(2,1)}), bf16[32,4,8192]{2,1,0:T(4,128)(2,1)S(1)}, u32[]{:S(2)}, u32[]{:S(2)}) async-start(bf16[32,4,8192]{2,1,0:T(4,128)(2,1)} %stack.9), calls=%async_computation.1 | async-start | bytes 4194304 | tf_op jit(solution)/shard_map/all_to_all | solution.py:45
  539.6 294.8 %all-reduce.19.cloned.1.call-start = ((), (), s32[]{:S(2)}) async-start(), calls=%async_computation.13 | async-start | bytes 4194304
  598.7 253.5 %copy-start.38 = (bf16[128,2,128]{0,2,1:T(8,128)(2,1)}, bf16[128,2,128]{0,2,1:T(8,128)(2,1)S(1)}, u32[]{:S(2)}) copy-start(bf16[128,2,128]{0,2,1:T(8,128)(2,1)S(1)} %get-tuple-element.28) | copy-start | bytes 196612
  599.9 252.3 %copy-start.27 = (f32[2,128,256]{1,2,0:T(8,128)}, f32[2,128,256]{1,2,0:T(8,128)S(1)}, u32[]{:S(2)}) copy-start(f32[2,128,256]{1,2,0:T(8,128)S(1)} %get-tuple-element.26) | copy-start | bytes 786436
  606.4 229.1 %copy-start.35 = (bf16[4,8192]{1,0:T(4,128)(2,1)S(1)}, bf16[4,8192]{1,0:T(4,128)(2,1)}, u32[]{:S(2)}) copy-start(bf16[4,8192]{1,0:T(4,128)(2,1)} %param.18) | copy-start | bytes 196612
  607.5 238.5 %copy-start.10 = (bf16[4,8192]{1,0:T(4,128)(2,1)}, bf16[4,8192]{1,0:T(4,128)(2,1)S(1)}, u32[]{:S(2)}) copy-start(bf16[4,8192]{1,0:T(4,128)(2,1)S(1)} %get-tuple-element.25) | copy-start | bytes 196612
  836.6 6.5 collective-permute-start.1
  846.0 55.6 %all-to-all-start.3 = ((bf16[32,4,8192]{2,1,0:T(4,128)(2,1)}), bf16[32,4,8192]{2,1,0:T(4,128)(2,1)}, u32[]{:S(2)}, u32[]{:S(2)}) async-start(bf16[32,4,8192]{2,1,0:T(4,128)(2,1)} %stack.11), calls=%async_computation.3 | async-start | bytes 4194304 | tf_op jit(solution)/shard_map/all_to_all | solution.py:45
  852.1 281.2 %all-reduce.15.cloned.1.call-start = ((), (), s32[]{:S(2)}) async-start(), calls=%async_computation.8 | async-start | bytes 2097152 | tf_op jit(solution)/shard_map/psum | solution.py:61
  912.1 246.9 %reduce-scatter.8.cloned.1.call-start = ((), (), s32[]{:S(2)}) async-start(), calls=%async_computation.11 | async-start | bytes 1310720 | tf_op jit(solution)/shard_map/reduce_scatter | solution.py:215
  1026.1 161.2 %reduce-scatter.6.cloned.1.call-start = ((), (), s32[]{:S(2)}) async-start(), calls=%async_computation.10 | async-start | bytes 1310720 | tf_op jit(solution)/shard_map/reduce_scatter | solution.py:214
  1138.7 287.7 %all-reduce.21.cloned.1.call-start = ((), (), s32[]{:S(2)}) async-start(), calls=%async_computation.14 | async-start | bytes 8388608
  1150.5 275.9 %copy-start.11 = (bf16[4,8192]{1,0:T(4,128)(2,1)S(1)}, bf16[4,8192]{1,0:T(4,128)(2,1)}, u32[]{:S(2)}) copy-start(bf16[4,8192]{1,0:T(4,128)(2,1)} %copy-done.10) | copy-start | bytes 196612
  1150.6 277.1 %copy-start.25 = (bf16[4,8192]{1,0:T(4,128)(2,1)S(1)}, bf16[4,8192]{1,0:T(4,128)(2,1)}, u32[]{:S(2)}) copy-start(bf16[4,8192]{1,0:T(4,128)(2,1)} %copy-done.23) | copy-start | bytes 196612
  1150.6 277.0 %copy-start.29 = (bf16[4,8192]{1,0:T(4,128)(2,1)S(1)}, bf16[4,8192]{1,0:T(4,128)(2,1)}, u32[]{:S(2)}) copy-start(bf16[4,8192]{1,0:T(4,128)(2,1)} %copy-done.28) | copy-start | bytes 196612
  1150.6 277.0 %copy-start.31 = (bf16[4,8192]{1,0:T(4,128)(2,1)S(1)}, bf16[4,8192]{1,0:T(4,128)(2,1)}, u32[]{:S(2)}) copy-start(bf16[4,8192]{1,0:T(4,128)(2,1)} %copy-done.30) | copy-start | bytes 196612
  1150.6 277.0 %copy-start.33 = (bf16[4,8192]{1,0:T(4,128)(2,1)S(1)}, bf16[4,8192]{1,0:T(4,128)(2,1)}, u32[]{:S(2)}) copy-start(bf16[4,8192]{1,0:T(4,128)(2,1)} %copy-done.32) | copy-start | bytes 196612
  1150.6 295.8 %reduce-scatter.4.cloned.1.call-start = ((), (), s32[]{:S(2)}) async-start(), calls=%async_computation.9 | async-start | bytes 393216 | tf_op jit(solution)/shard_map/reduce_scatter | solution.py:208
  (33 other events, 342.4 us)
Sparse Core Ops, SparseCore 0:
  15.2 245.0 all-reduce.12
  289.4 235.8 all-reduce.16
  606.6 227.7 all-reduce.18
  912.2 221.1 all-reduce.14
  1135.7 23.1 reduce-scatter.7
  1161.5 25.8 reduce-scatter.5
  1190.1 236.3 all-reduce.20
  1429.5 16.8 reduce-scatter.3
